TPU v7x, 32 devices: a whole 2x2x4 slice. The times are simulated.
32 devices in a mesh: lat: 4 (over y, x), lon: 8 (over z, core).
Axes of the slice: x: 2, y: 2, z: 4, core: 2. Of those that a mesh axis runs over, the one named last changes fastest.
Arguments:
- field: bfloat16 [4, 70, 128, 256], P(None, None, 'lat', 'lon'), may hold values from -6 to 6
- embed_weight: bfloat16 [1536, 1120], P(('lat', 'lon')), may hold values from -0.1875 to 0.1875
- embed_bias: float32 [1536], replicated, may hold values from -3 to 3
- embed_gain: float32 [1536], replicated, may hold values from 0.1 to 1.9
- embed_shift: float32 [1536], replicated, may hold values from -2 to 2
- qkv_weight: bfloat16 [1536, 2304], P(('lat', 'lon')), may hold values from -0.15625 to 0.15625
- logit_scale: float32 [12], replicated, may hold values from 1.6 to 5
- bias_table: float32 [12, 15, 15], replicated, may hold values from -6 to 6
- proj_weight: bfloat16 [1536, 768], P(('lat', 'lon')), may hold values from -0.21875 to 0.21875
- post_gain: float32 [1536], replicated, may hold values from 0.1 to 1.9
- post_shift: float32 [1536], replicated, may hold values from -2 to 2
Outputs:
- block_out: bfloat16 [4, 32, 64, 1536], P(None, 'lat', 'lon')
All inputs are finite; a program needn't handle non-finite values.
Results may differ from a plain program's by a relative error of at most 0.011.
Values may be sent and summed in bfloat16 or wider, within the bound.
A program may use at most 128 MiB of HBM per device.

v0:
```python
import math

import jax
import jax.numpy as jnp
from jax import lax
from jax.sharding import PartitionSpec as P

VARS = 70
PATCH = 4
D = 1536
HEADS = 12
HD = 64
WIN = 8


scale_cap = math.log(100.0)


def shifted(value, axis, steps):
    count = lax.axis_size(axis)
    pairs = [(source, (source + steps) % count) for source in range(count)]
    return lax.ppermute(value, axis, pairs)


def layer_norm(inputs, gain, shift):
    average = jnp.mean(inputs, axis=-1, keepdims=True)
    centred = inputs - average
    spread = jnp.mean(centred * centred, axis=-1, keepdims=True)
    return centred * lax.rsqrt(spread + 1e-05) * gain + shift


def dot_rows(left, right):
    return lax.dot_general(
        left, right, (((1,), (1,)), ((), ())), preferred_element_type=jnp.float32
    )


def window_bias(bias_table, window):
    places = jnp.arange(window * window, dtype=jnp.int32)
    row_place = places // window
    col_place = places % window
    row_gap = row_place[:, None] - row_place[None, :] + window - 1
    col_gap = col_place[:, None] - col_place[None, :] + window - 1
    levels = jnp.arange(2 * window - 1, dtype=jnp.int32)
    row_onehot = (row_gap[:, :, None] == levels).astype(jnp.float32)
    col_onehot = (col_gap[:, :, None] == levels).astype(jnp.float32)
    table = 16.0 * jax.nn.sigmoid(bias_table)
    by_rows = jnp.einsum("hrc,qkc->hqkr", table, col_onehot, precision=lax.Precision.HIGHEST)
    return jnp.sum(by_rows * row_onehot[None], axis=-1)


def cosine_unit(inputs):
    widened = inputs.astype(jnp.float32)
    total = jnp.sum(widened * widened, axis=-1, keepdims=True)
    return (widened * lax.rsqrt(total + 1e-06)).astype(jnp.bfloat16)


def to_windows(grid_block, window):
    batch, row_count, col_count, features = grid_block.shape
    shaped = grid_block.reshape(
        batch, row_count // window, window, col_count // window, window, features
    )
    return shaped.transpose(0, 1, 3, 2, 4, 5).reshape(-1, window * window, features)


def from_windows(windowed, batch, row_count, col_count, window):
    features = windowed.shape[-1]
    shaped = windowed.reshape(
        batch, row_count // window, col_count // window, window, window, features
    )
    return shaped.transpose(0, 1, 3, 2, 4, 5).reshape(batch, row_count, col_count, features)


def attend(query_block, kv_block, row_groups, scales, bias):
    batch, row_count, col_count = (query_block.shape[0], query_block.shape[1], query_block.shape[2])
    inner = HEADS * HD
    query_win = to_windows(query_block, WIN).reshape(-1, WIN * WIN, HEADS, HD)
    kv_win = to_windows(kv_block, WIN).reshape(-1, WIN * WIN, 2, HEADS, HD)
    groups = jnp.broadcast_to(
        row_groups.reshape(1, row_count // WIN, 1, WIN, 1),
        (batch, row_count // WIN, col_count // WIN, WIN, WIN),
    ).reshape(-1, WIN * WIN)
    q_unit = cosine_unit(query_win)
    k_unit = cosine_unit(kv_win[:, :, 0])
    scores = jnp.einsum("wqhd,wkhd->whqk", q_unit, k_unit, preferred_element_type=jnp.float32)
    scores = scores * scales[None, :, None, None] + bias[None]
    allowed = groups[:, :, None] == groups[:, None, :]
    scores = jnp.where(allowed[:, None], scores, jnp.float32(-1e30))
    highest = jnp.max(scores, axis=-1, keepdims=True)
    expo = jnp.exp(scores - highest)
    weights = (expo / jnp.sum(expo, axis=-1, keepdims=True)).astype(jnp.bfloat16)
    attended = jnp.einsum(
        "whqk,wkhd->wqhd", weights, kv_win[:, :, 1], preferred_element_type=jnp.float32
    )
    attended = attended.astype(jnp.bfloat16).reshape(-1, WIN * WIN, inner)
    return from_windows(attended, batch, row_count, col_count, WIN)


def rolled_groups(band_start, tile_rows, lat_total, offset):
    rolled_rows = band_start + jnp.arange(tile_rows, dtype=jnp.int32)
    global_rows = (rolled_rows + offset) % lat_total
    return jnp.where(global_rows < offset, -1, (global_rows - offset) // WIN)


def on_device(
    field,
    embed_weight,
    embed_bias,
    embed_gain,
    embed_shift,
    qkv_weight,
    logit_scale,
    bias_table,
    proj_weight,
    post_gain,
    post_shift,
):
    batch = field.shape[0]
    tile_rows = field.shape[2] // PATCH
    tile_cols = field.shape[3] // PATCH
    patch_len = VARS * PATCH * PATCH
    offset = WIN // 2
    inner = HEADS * HD
    lat_total = tile_rows * lax.axis_size("lat")
    band_start = lax.axis_index("lat") * tile_rows
    scales = jnp.exp(jnp.minimum(logit_scale, scale_cap))
    bias = window_bias(bias_table, WIN)
    patches = (
        field.reshape(batch, VARS, tile_rows, PATCH, tile_cols, PATCH)
        .transpose(0, 2, 4, 1, 3, 5)
        .reshape(batch * tile_rows * tile_cols, patch_len)
    )
    embed_band, qkv_band, proj_band = (
        lax.all_gather(embed_weight, "lon", axis=0, tiled=True),
        lax.all_gather(qkv_weight, "lon", axis=0, tiled=True),
        lax.all_gather(proj_weight, "lon", axis=0, tiled=True),
    )
    embed_pre = dot_rows(patches, lax.all_gather(embed_band, "lat", axis=0, tiled=True))
    tokens = layer_norm(embed_pre + embed_bias, embed_gain, embed_shift).astype(jnp.bfloat16)
    tokens = tokens.reshape(batch, tile_rows, tile_cols, D)
    lat_recv = shifted(tokens[:, :offset], "lat", -1)
    rolled = jnp.concatenate([tokens[:, offset:], lat_recv], axis=1)
    lon_recv = shifted(rolled[:, :, :offset], "lon", -1)
    rolled = jnp.concatenate([rolled[:, :, offset:], lon_recv], axis=2)
    flat_tokens = rolled.reshape(-1, D)
    product = jnp.dot(
        flat_tokens,
        lax.all_gather(qkv_band, "lat", axis=0, tiled=True),
        preferred_element_type=jnp.float32,
    )
    qkv = product.astype(jnp.bfloat16).reshape(batch, tile_rows, tile_cols, 3 * inner)
    row_groups = rolled_groups(band_start, tile_rows, lat_total, offset)
    attended = attend(qkv[..., :inner], qkv[..., inner:], row_groups, scales, bias)
    flat_attended = attended.reshape(-1, inner)
    projected = dot_rows(flat_attended, lax.all_gather(proj_band, "lat", axis=0, tiled=True))
    mixed = rolled.reshape(-1, D).astype(jnp.float32) + layer_norm(projected, post_gain, post_shift)
    mixed = mixed.astype(jnp.bfloat16).reshape(batch, tile_rows, tile_cols, D)
    lat_back = shifted(mixed[:, tile_rows - offset :], "lat", 1)
    mixed = jnp.concatenate([lat_back, mixed[:, : tile_rows - offset]], axis=1)
    lon_back = shifted(mixed[:, :, tile_cols - offset :], "lon", 1)
    mixed = jnp.concatenate([lon_back, mixed[:, :, : tile_cols - offset]], axis=2)
    return mixed


def solution(mesh):
    placed = (
        P(None, None, "lat", "lon"),
        P(("lat", "lon"), None),
        P(),
        P(),
        P(),
        P(("lat", "lon"), None),
        P(),
        P(),
        P(("lat", "lon"), None),
        P(),
        P(),
    )
    return jax.shard_map(
        on_device,
        mesh=mesh,
        in_specs=placed,
        out_specs=P(None, "lat", "lon", None),
        check_vma=False,
    )
```

profile of v0, /device:TPU:0, one launch (start us, length us, event | category | flops | bytes accessed | tf_op | source)
XLA Modules:
  0.0 242.4 jit_solution(3552394309512701030)
XLA Ops:
  6.5 0.7 all-gather.7.cloned.1.call-update
  7.3 0.0 all-gather.5.cloned.1.call-start
  7.3 20.4 %all_gather.18 = bf16[384,1120]{1,0:T(8,128)(2,1)} all-gather(bf16[48,1120]{1,0:T(8,128)(2,1)} %param.12), channel_id=1, replica_groups=mesh['lat'=4,'lon'=8] {'lon'}, dimensions={0}, use_global_device_ids=true | all-gather | bytes 967680 | tf_op jit(solution)/shard_map/all_gather | solution.py:134
  27.7 0.0 all-gather.5.cloned.1.call-update
  27.7 0.0 all-gather.9.cloned.1.call-start
  27.8 12.2 %all-gather.7.cloned.1.call-done = bf16[384,2304]{1,0:T(8,128)(2,1)} async-done(((bf16[48,2304]{1,0:T(8,128)(2,1)}), bf16[384,2304]{1,0:T(8,128)(2,1)}) %all-gather.7.cloned.1.call-update) | async-done | bytes 1769488 | tf_op jit(solution)/shard_map/all_gather | solution.py:135
  40.0 0.0 all-gather.9.cloned.1.call-update
  40.0 0.0 all-gather.11.cloned.1.call-start
  40.1 15.9 %all_gather.22 = bf16[384,768]{1,0:T(8,128)(2,1)} all-gather(bf16[48,768]{1,0:T(8,128)(2,1)S(1)} %copy-done.5), channel_id=1, replica_groups=mesh['lat'=4,'lon'=8] {'lon'}, dimensions={0}, use_global_device_ids=true | all-gather | bytes 663552 | tf_op jit(solution)/shard_map/all_gather | solution.py:136
  56.0 0.0 all-gather.11.cloned.1.call-update
  56.1 15.0 %copy.30 = bf16[4,70,8,4,8,4]{4,2,0,5,3,1:T(8,128)(2,1)} copy(bf16[4,70,8,4,8,4]{1,5,4,3,2,0:T(4,128)(2,1)S(1)} %bitcast.52) | data formatting | bytes 1146880 | tf_op jit(solution)/shard_map/reshape | solution.py:129
  71.0 13.1 %reshape.213 = bf16[256,1120]{0,1:T(8,128)(2,1)S(1)} reshape(bf16[4,8,8,70,4,4]{2,1,0,5,4,3:T(8,128)(2,1)} %bitcast.46) | data formatting | bytes 1146880 | tf_op jit(solution)/shard_map/reshape | solution.py:131
  84.2 0.1 subtract_add_fusion
  84.3 4.1 %all-gather.5.cloned.1.call-done = bf16[1536,1120]{1,0:T(8,128)(2,1)} async-done(((bf16[384,1120]{1,0:T(8,128)(2,1)}), bf16[1536,1120]{1,0:T(8,128)(2,1)}) %all-gather.5.cloned.1.call-update) | async-done | bytes 3440656 | tf_op jit(solution)/shard_map/all_gather | solution.py:138
  88.4 3.3 %fusion.31 = (f32[256]{0:T(256)S(1)}, f32[256,1536]{1,0:T(8,128)S(1)}) fusion(f32[1536]{0:T(1024)S(1)} %copy-done.12, bf16[256,1120]{0,1:T(8,128)(2,1)S(1)} %reshape.213, bf16[1536,1120]{1,0:T(8,128)(2,1)} %all-gather.5.cloned.1.call-done), kind=kOutput, calls=%fused_computation.78 | convolution fusion | flops 881590016 | bytes 5594112 | tf_op jit(solution)/shard_map/dot_general | solution.py:33
  91.7 0.3 multiply_reduce_fusion.3
  92.0 0.4 copy-done.7
  92.4 0.3 add_convert_fusion.1
  92.8 0.1 fusion.30
  92.8 1.5 collective-permute-start
  94.3 0.1 subtract_add_fusion.1
  94.4 4.0 %multiply_reduce_fusion = f32[64,64,12]{1,2,0:T(8,128)S(1)} fusion(f32[64,64,15]{1,2,0:T(8,128)S(1)} %fusion.13, s32[64,64]{1,0:T(8,128)S(1)} %subtract_add_fusion.1, f32[12,15,15]{2,1,0:T(8,128)S(1)} %copy-done.11), kind=kOutput, calls=%fused_computation.1 | convolution fusion | flops 134208048 | bytes 469552 | tf_op jit(solution)/shard_map/hrc,qkc->hqkr/dot_general | solution.py:48
  98.5 0.2 copy.34
  98.7 0.1 broadcast_in_dim.17
  98.8 0.1 broadcast_in_dim.18
  98.9 8.1 %collective-permute-done = bf16[4,4,8,1536]{3,2,1,0:T(8,128)(2,1)S(1)} collective-permute-done((bf16[4,4,8,1536]{3,2,1,0:T(8,128)(2,1)S(1)}, bf16[4,4,8,1536]{3,2,1,0:T(8,128)(2,1)S(1)}, u32[]{:S(2)}, u32[]{:S(2)}) %collective-permute-start) | collective-permute-done | bytes 393248 | tf_op jit(solution)/shard_map/ppermute | solution.py:22
  107.0 0.3 fusion.15
  107.3 0.2 collective-permute-start.1
  107.5 0.7 broadcast_compare_fusion
  108.2 4.6 %collective-permute-done.1 = bf16[4,8,4,1536]{3,2,1,0:T(4,128)(2,1)S(1)} collective-permute-done((bf16[4,8,4,1536]{3,2,1,0:T(4,128)(2,1)S(1)}, bf16[4,8,4,1536]{3,2,1,0:T(4,128)(2,1)S(1)}, u32[]{:S(2)}, u32[]{:S(2)}) %collective-permute-start.1) | collective-permute-done | bytes 393248 | tf_op jit(solution)/shard_map/ppermute | solution.py:22
  112.8 0.4 pad_maximum_fusion.1
  113.2 56.5 %all-gather.9.cloned.1.call-done = bf16[1536,2304]{1,0:T(8,128)(2,1)} async-done(((bf16[384,2304]{1,0:T(8,128)(2,1)}), bf16[1536,2304]{1,0:T(8,128)(2,1)}) %all-gather.9.cloned.1.call-update) | async-done | bytes 7077904 | tf_op jit(solution)/shard_map/all_gather | solution.py:148
  169.7 5.0 %convolution_convert_fusion = bf16[256,2304]{1,0:T(8,128)(2,1)S(1)} fusion(bf16[256,1536]{1,0:T(8,128)(2,1)S(1)} %bitcast.47, bf16[1536,2304]{1,0:T(8,128)(2,1)} %all-gather.9.cloned.1.call-done), kind=kOutput, calls=%fused_computation.2 | convolution fusion | flops 1812529152 | bytes 9043968 | tf_op jit(solution)/shard_map/dot_general | solution.py:146
  174.7 0.1 slice.52
  174.8 2.8 %reshape_reshape_transpose_reshape.4 = bf16[4,64,2,12,64]{4,3,2,1,0:T(8,128)(2,1)} reshape(bf16[4,8,8,1536]{3,2,1,0:T(8,128)(2,1)S(1)} %slice.52) | data formatting | bytes 1572864 | tf_op jit(solution)/shard_map/reshape;reshape;transpose;reshape | solution.py:78
  177.6 0.1 slice_convert_fusion
  177.7 0.5 reshape.218
  178.1 1.3 slice-done
  179.5 1.5 copy.41
  181.0 1.8 fusion.1
  182.9 0.6 multiply_reduce_fusion.1
  183.5 0.9 copy-done
  184.4 1.3 fusion.2
  185.7 0.6 add_select_fusion
  186.3 1.1 copy-done.14
  187.4 0.4 fusion.32
  187.8 0.7 copy-done.4
  188.6 2.4 fusion.5
  191.0 0.6 copy.36
  191.6 0.5 reshape_reshape_transpose_reshape_reshape.3
  192.1 16.8 %all-gather.11.cloned.1.call-done = bf16[1536,768]{1,0:T(8,128)(2,1)} async-done(((bf16[384,768]{1,0:T(8,128)(2,1)}), bf16[1536,768]{1,0:T(8,128)(2,1)}) %all-gather.11.cloned.1.call-update) | async-done | bytes 2359312 | tf_op jit(solution)/shard_map/all_gather | solution.py:155
  208.9 2.6 %fusion.33 = (f32[256]{0:T(256)S(1)}, f32[256,1536]{1,0:T(8,128)S(1)}) fusion(bf16[256,768]{0,1:T(8,128)(2,1)S(1)} %reshape_reshape_transpose_reshape_reshape.3, bf16[1536,768]{1,0:T(8,128)(2,1)} %all-gather.11.cloned.1.call-done), kind=kOutput, calls=%fused_computation.80 | convolution fusion | flops 604372736 | bytes 4326400 | tf_op jit(solution)/shard_map/dot_general | solution.py:33
  211.5 0.3 multiply_reduce_fusion.2
  211.8 0.8 copy-done.2
  212.6 0.5 add_convert_fusion
  213.1 0.1 fusion.29
  213.1 1.5 collective-permute-start.2
  214.7 10.3 %collective-permute-done.2 = bf16[4,4,8,1536]{3,2,1,0:T(8,128)(2,1)S(1)} collective-permute-done((bf16[4,4,8,1536]{3,2,1,0:T(8,128)(2,1)S(1)}, bf16[4,4,8,1536]{3,2,1,0:T(8,128)(2,1)S(1)}, u32[]{:S(2)}, u32[]{:S(2)}) %collective-permute-start.2) | collective-permute-done | bytes 393248 | tf_op jit(solution)/shard_map/ppermute | solution.py:22
  225.0 0.3 fusion.14
  225.3 0.1 copy.37
  225.3 0.1 collective-permute-start.3
  225.4 9.0 %collective-permute-done.3 = bf16[4,8,4,1536]{3,1,2,0:T(8,128)(2,1)S(1)} collective-permute-done((bf16[4,8,4,1536]{3,1,2,0:T(8,128)(2,1)S(1)}, bf16[4,8,4,1536]{3,1,2,0:T(8,128)(2,1)S(1)}, u32[]{:S(2)}, u32[]{:S(2)}) %collective-permute-start.3) | collective-permute-done | bytes 393248 | tf_op jit(solution)/shard_map/ppermute | solution.py:22
  234.4 0.2 copy.38
  234.6 1.2 fusion.6
  (38 shorter events, 0.2 us)
Async XLA Ops:
  6.5 33.5 %all-gather.7.cloned.1.call-start = ((), (), s32[]{:S(2)}) async-start(), calls=%async_computation.1 | async-start | bytes 1990656 | tf_op jit(solution)/shard_map/all_gather | solution.py:135
  7.3 81.1 %all-gather.5.cloned.1.call-start = ((), (), s32[]{:S(2)}) async-start(), calls=%async_computation | async-start | bytes 4423680 | tf_op jit(solution)/shard_map/all_gather | solution.py:138
  27.7 12.4 %copy-start.5 = (bf16[48,768]{1,0:T(8,128)(2,1)S(1)}, bf16[48,768]{1,0:T(8,128)(2,1)}, u32[]{:S(2)}) copy-start(bf16[48,768]{1,0:T(8,128)(2,1)} %param.19) | copy-start | bytes 221188
  27.7 28.3 %copy-start.3 = (bf16[4,70,32,32]{1,3,2,0:T(8,128)(2,1)S(1)}, bf16[4,70,32,32]{1,3,2,0:T(8,128)(2,1)}, u32[]{:S(2)}) copy-start(bf16[4,70,32,32]{1,3,2,0:T(8,128)(2,1)} %param.11) | copy-start | bytes 1720324
  27.7 141.9 %all-gather.9.cloned.1.call-start = ((), (), s32[]{:S(2)}) async-start(), calls=%async_computation.2 | async-start | bytes 8847360 | tf_op jit(solution)/shard_map/all_gather | solution.py:148
  40.0 168.9 %all-gather.11.cloned.1.call-start = ((), (), s32[]{:S(2)}) async-start(), calls=%async_computation.3 | async-start | bytes 2949120 | tf_op jit(solution)/shard_map/all_gather | solution.py:155
  71.0 17.3 %copy-start.12 = (f32[1536]{0:T(1024)S(1)}, f32[1536]{0:T(1024)}, u32[]{:S(2)}) copy-start(f32[1536]{0:T(1024)} %param.13) | copy-start | bytes 18436
  91.7 0.7 copy-start.7
  91.7 0.7 copy-start.8
  92.4 2.0 copy-start.11
  92.8 14.2 %collective-permute-start = (bf16[4,4,8,1536]{3,2,1,0:T(8,128)(2,1)S(1)}, bf16[4,4,8,1536]{3,2,1,0:T(8,128)(2,1)S(1)}, u32[]{:S(2)}, u32[]{:S(2)}) collective-permute-start(bf16[4,4,8,1536]{3,2,1,0:T(8,128)(2,1)S(1)} %get-tuple-element.10), channel_id=1, source_target_pairs={{0,24},{8,0},{16,8},{24,16},{1,25},{9,1},{17,9},{25,17},{2,26},{10... | collective-permute-start | bytes 1179656 | tf_op jit(solution)/shard_map/ppermute | solution.py:22
  98.5 9.1 %copy-start.13 = (f32[12]{0:T(128)S(1)}, f32[12]{0:T(128)}, u32[]{:S(2)}) copy-start(f32[12]{0:T(128)} %param.17) | copy-start | bytes 148
  107.3 5.5 %collective-permute-start.1 = (bf16[4,8,4,1536]{3,2,1,0:T(4,128)(2,1)S(1)}, bf16[4,8,4,1536]{3,2,1,0:T(4,128)(2,1)S(1)}, u32[]{:S(2)}, u32[]{:S(2)}) collective-permute-start(bf16[4,8,4,1536]{3,2,1,0:T(4,128)(2,1)S(1)} %get-tuple-element.8), channel_id=1, source_target_pairs={{0,7},{1,0},{2,1},{3,2},{4,3},{5,4},{6,5},{7,6},{8,15},{9,8},{10,9... | collective-permute-start | bytes 1179656 | tf_op jit(solution)/shard_map/ppermute | solution.py:22
  113.2 61.5 %copy-start.1 = (bf16[4,8,8,1536]{3,2,1,0:T(8,128)(2,1)}, bf16[4,8,8,1536]{3,2,1,0:T(8,128)(2,1)S(1)}, u32[]{:S(2)}) copy-start(bf16[4,8,8,1536]{3,2,1,0:T(8,128)(2,1)S(1)} %pad_maximum_fusion.1) | copy-start | bytes 2359300
  178.1 1.3 slice-start
  182.9 1.6 copy-start
  184.4 1.3 copy-start.6
  186.3 1.1 copy-start.14
  187.4 1.1 copy-start.4
  211.5 1.1 copy-start.2
  211.5 1.1 copy-start.9
  211.5 1.1 copy-start.10
  213.1 11.8 %collective-permute-start.2 = (bf16[4,4,8,1536]{3,2,1,0:T(8,128)(2,1)S(1)}, bf16[4,4,8,1536]{3,2,1,0:T(8,128)(2,1)S(1)}, u32[]{:S(2)}, u32[]{:S(2)}) collective-permute-start(bf16[4,4,8,1536]{3,2,1,0:T(8,128)(2,1)S(1)} %get-tuple-element.5), channel_id=1, source_target_pairs={{0,8},{8,16},{16,24},{24,0},{1,9},{9,17},{17,25},{25,1},{2,10},{10... | collective-permute-start | bytes 1179656 | tf_op jit(solution)/shard_map/ppermute | solution.py:22
  225.3 9.1 %collective-permute-start.3 = (bf16[4,8,4,1536]{3,1,2,0:T(8,128)(2,1)S(1)}, bf16[4,8,4,1536]{3,1,2,0:T(8,128)(2,1)S(1)}, u32[]{:S(2)}, u32[]{:S(2)}) collective-permute-start(bf16[4,8,4,1536]{3,1,2,0:T(8,128)(2,1)S(1)} %copy.37), channel_id=1, source_target_pairs={{0,1},{1,2},{2,3},{3,4},{4,5},{5,6},{6,7},{7,0},{8,9},{9,10},{10,1... | collective-permute-start | bytes 1179656 | tf_op jit(solution)/shard_map/ppermute | solution.py:22
Sparse Core Ops, SparseCore 0:
  9.0 30.9 all-gather.6
  41.8 46.4 all-gather.4
  90.2 79.4 all-gather.8
  171.4 37.4 all-gather.10
where the time goes:
time: 243 us; the launch traced here: 242 us
  waiting for transfers between devices  122 us (50%)
  local copies, waits for them, and re-layouts  40.2 us (17%)
  blocking collectives  36.3 us (15%)
  matrix products  17.9 us (7%)
  between operations  13.5 us (6%)
  other arithmetic  8.76 us (4%)
  starting transfers between devices  3.45 us (1%)
    all_gather x1, waiting for transfers between devices, on_device(): lax.all_gather(qkv_band, 'lat', axis=0, tiled=True)  56.5 us
    ppermute x4, waiting for transfers between devices, shifted(): return lax.ppermute(value, axis, pairs)  32 us
    all_gather x1, blocking collectives, on_device(): lax.all_gather(embed_weight, 'lon', axis=0, tiled=True)  20.4 us
    all_gather x1, waiting for transfers between devices, on_device(): lax.all_gather(proj_band, 'lat', axis=0, tiled=True)  16.8 us
    all_gather x1, blocking collectives, on_device(): lax.all_gather(proj_weight, 'lon', axis=0, tiled=True)  15.9 us
    reshape x1, local copies, waits for them, and re-layouts, on_device(): field.reshape(batch, VARS, tile_rows, PATCH, tile_cols, PATCH)  15 us
    reshape x1, local copies, waits for them, and re-layouts, on_device(): patches = field.reshape(batch, VARS, tile_rows, PATCH, tile_cols, PATCH)....  13.1 us
    all_gather x1, waiting for transfers between devices, on_device(): lax.all_gather(qkv_weight, 'lon', axis=0, tiled=True)  12.2 us
  transfers between devices with their start and end apart: 8, of which 8 were waited for; matrix products, arithmetic and copies ran while one was open for 23% of the time, Pallas kernels for 0%

commit v1 on v0

v1 whole, which is shorter than its diff:
```python
import functools
import math

import jax
import jax.numpy as jnp
from jax import lax
from jax.experimental import pallas as pl
from jax.experimental.pallas import tpu as pltpu
from jax.sharding import PartitionSpec as P

VARS = 70
PATCH = 4
D = 1536
HEADS = 12
HD = 64
WIN = 8
HALF = WIN // 2
QUADS = 4
INNER = HEADS * HD

MESH = pl.DeviceIdType.MESH
VMEM_BYTES = 56 * 1024 * 1024

scale_cap = math.log(100.0)


def layer_norm(inputs, gain, shift):
    average = jnp.mean(inputs, axis=-1, keepdims=True)
    centred = inputs - average
    spread = jnp.mean(centred * centred, axis=-1, keepdims=True)
    return centred * lax.rsqrt(spread + 1e-05) * gain + shift


def dot_rows(left, right):
    return lax.dot_general(
        left, right, (((1,), (1,)), ((), ())), preferred_element_type=jnp.float32
    )


def dot_plain(left, right):
    return lax.dot_general(
        left, right, (((1,), (0,)), ((), ())), preferred_element_type=jnp.float32
    )


def iota(shape, dim):
    return lax.broadcasted_iota(jnp.int32, shape, dim)


def onehot(condition):
    return jnp.where(condition, 1.0, 0.0).astype(jnp.bfloat16)


def window_bias(bias_table):
    places = jnp.arange(WIN * WIN, dtype=jnp.int32)
    quad, rest = places // 16, places % 16
    row_place = quad // 2 * HALF + rest // HALF
    col_place = quad % 2 * HALF + rest % HALF
    row_gap = row_place[:, None] - row_place[None, :] + WIN - 1
    col_gap = col_place[:, None] - col_place[None, :] + WIN - 1
    levels = jnp.arange(2 * WIN - 1, dtype=jnp.int32)
    row_onehot = (row_gap[:, :, None] == levels).astype(jnp.float32)
    col_onehot = (col_gap[:, :, None] == levels).astype(jnp.float32)
    table = 16.0 * jax.nn.sigmoid(bias_table)
    by_rows = jnp.einsum("hrc,qkc->hqkr", table, col_onehot, precision=lax.Precision.HIGHEST)
    return jnp.sum(by_rows * row_onehot[None], axis=-1)


def patch_kernel(field_ref, out_ref, spread):
    batch = field_ref.shape[0]
    spread[...] = jnp.zeros_like(spread)
    side = WIN * PATCH
    pick_row = iota((side, side), 0)
    pick_col = iota((side, side), 1)
    pick = onehot(pick_col == (pick_row % WIN) * PATCH + pick_row // WIN)
    for sample in range(batch):
        for row in range(side):
            i, p = row // PATCH, row % PATCH
            picked = dot_rows(pick, field_ref[sample, row])
            for q in range(PATCH):
                lane = (p * PATCH + q) * 128
                spread[pl.ds((sample * WIN + i) * WIN, WIN), lane : lane + VARS] = picked[
                    q * WIN : (q + 1) * WIN
                ]
    tokens = batch * WIN * WIN
    to = iota((tokens, tokens), 0)
    source = iota((tokens, tokens), 1)
    per_quad = batch * 16
    quad, sample, place = to // per_quad, to % per_quad // 16, to % 16
    row = quad // 2 * HALF + place // HALF
    col = quad % 2 * HALF + place % HALF
    order = onehot(source == (sample * WIN + row) * WIN + col)
    length = VARS * PATCH * PATCH
    feature = iota((128, length), 1)
    same = feature // 16 == iota((128, length), 0)
    slot = feature % 16
    total = jnp.zeros((tokens, length), jnp.float32)
    for pq in range(16):
        piece = spread[:, pq * 128 : (pq + 1) * 128].astype(jnp.bfloat16)
        total = total + dot_plain(piece, onehot(same & (slot == pq)))
    out = dot_plain(order, total.astype(jnp.bfloat16)).astype(jnp.bfloat16)
    out_ref[...] = out.reshape(out_ref.shape)


def exchange_kernel(lat_size, lon_size, weights, patch_ref, *refs):
    local, outs = refs[:weights], refs[weights + 1 : 2 * weights + 1]
    rolled = refs[weights]
    send_sem, recv_sem, own_sem = refs[2 * weights + 1 :]
    lat, lon = lax.axis_index("lat"), lax.axis_index("lon")
    before = (lax.rem(lat + lat_size - 1, lat_size), lax.rem(lon + lon_size - 1, lon_size))
    after = (lax.rem(lat + 1, lat_size), lax.rem(lon + 1, lon_size))
    targets = [(lat, before[1]), (before[0], lon), (before[0], before[1])]
    sources = [(lat, after[1]), (after[0], lon), (after[0], after[1])]
    y, x = lat // 2, lax.rem(lat, 2)
    z, core = lon // 2, lax.rem(lon, 2)
    peers = []
    if weights:
        depth = lon_size // 2
        lat_x = y * 2 + 1 - x
        lat_y = (1 - y) * 2 + x
        lat_d = (1 - y) * 2 + 1 - x
        other = z * 2 + 1 - core

        def lon_at(k):
            return lax.rem(z + depth - k, depth) * 2 + core

        to_x, to_y, to_c = (lat_x, lon), (lat_y, lon), (lat, other)
        to_z = [(lat, lax.rem(z + k, depth) * 2 + core) for k in range(depth)]
        peers = [to_x, to_y, to_c] + to_z[1:]
    barrier = pltpu.get_barrier_semaphore()
    greeted = targets + sources + peers
    for peer in greeted:
        pl.semaphore_signal(barrier, inc=1, device_id=peer, device_id_type=MESH)
    pl.semaphore_wait(barrier, len(greeted))

    count = [0]
    started = []

    def send(src, dst, landing, device):
        index = count[0]
        count[0] += 1
        copy = pltpu.make_async_remote_copy(
            src_ref=src, dst_ref=dst, send_sem=send_sem.at[index], recv_sem=recv_sem.at[index],
            device_id=device, device_id_type=MESH,
        )
        copy.start()
        started.append(copy)
        return pltpu.make_async_remote_copy(
            src_ref=src, dst_ref=landing, send_sem=send_sem.at[index], recv_sem=recv_sem.at[index],
            device_id=device, device_id_type=MESH,
        )

    arrivals = []
    for slot in (1, 2, 3):
        arrivals.append(
            send(patch_ref.at[3 - slot], rolled.at[slot], rolled.at[slot], targets[slot - 1])
        )
    keeps = [pltpu.make_async_copy(patch_ref.at[3], rolled.at[0], own_sem.at[0])]
    if weights:
        me = lat * lon_size + lon
        for t in range(weights):
            keeps.append(pltpu.make_async_copy(local[t], outs[t].at[me], own_sem.at[t + 1]))
    for keep in keeps:
        keep.start()
    if weights:

        def at(row, k, own=True):
            return row * lon_size + (lon_at(k) if own else lax.rem(z + depth - k, depth) * 2 + 1 - core)

        z_in, x_in, y_in = {}, {}, {}

        def fan(t, k, src):
            dst = outs[t].at[at(lat, k)]
            x_in[t, k] = send(src, dst, outs[t].at[at(lat_x, k)], to_x)
            y_in[t, k] = send(src, dst, outs[t].at[at(lat_y, k)], to_y)
            arrivals.append(send(src, dst, outs[t].at[at(lat, k, False)], to_c))

        for t in range(weights):
            for k in range(1, depth):
                z_in[t, k] = send(local[t], outs[t].at[me], outs[t].at[at(lat, k)], to_z[k])
            fan(t, 0, local[t])
        for t in range(weights):
            rows = local[t].shape[0]
            d_in = {}
            for k in range(1, depth):
                z_in[t, k].wait_recv()
                fan(t, k, outs[t].at[at(lat, k)])
            for k in range(depth):
                cut = rows // 3 // 16 * 16 * (1 + k % 2)
                x_in[t, k].wait_recv()
                block = outs[t].at[at(lat_x, k)]
                first = block.at[0:cut]
                d_one = send(first, first, outs[t].at[at(lat_d, k)].at[0:cut], to_y)
                arrivals.append(send(block, block, outs[t].at[at(lat_x, k, False)], to_c))
                y_in[t, k].wait_recv()
                block = outs[t].at[at(lat_y, k)]
                second = block.at[cut:rows]
                d_two = send(second, second, outs[t].at[at(lat_d, k)].at[cut:rows], to_x)
                arrivals.append(send(block, block, outs[t].at[at(lat_y, k, False)], to_c))
                d_in[k] = (d_one, d_two)
            for k in range(depth):
                for half in d_in[k]:
                    half.wait_recv()
                block = outs[t].at[at(lat_d, k)]
                arrivals.append(send(block, block, outs[t].at[at(lat_d, k, False)], to_c))
    for keep in keeps:
        keep.wait()
    for copy in arrivals:
        copy.wait_recv()
    for copy in started:
        copy.wait_send()


def exchange(mesh_shape, patches, tensors):
    lat_size, lon_size = mesh_shape
    weights = len(tensors)
    devices = lat_size * lon_size
    depth = lon_size // 2
    copies = 3 + weights * (depth - 1 + 2 * depth + 2 * depth + 4 * depth)
    anywhere = pl.BlockSpec(memory_space=pl.ANY)
    return pl.pallas_call(
        functools.partial(exchange_kernel, lat_size, lon_size, weights),
        out_shape=[jax.ShapeDtypeStruct(patches.shape, patches.dtype)]
        + [jax.ShapeDtypeStruct((devices,) + t.shape, t.dtype) for t in tensors],
        in_specs=[anywhere] * (1 + weights),
        out_specs=[anywhere] * (1 + weights),
        scratch_shapes=[
            pltpu.SemaphoreType.DMA((copies,)),
            pltpu.SemaphoreType.DMA((copies,)),
            pltpu.SemaphoreType.DMA((1 + weights,)),
        ],
        compiler_params=pltpu.CompilerParams(collective_id=0, has_side_effects=True),
    )(patches, *tensors)


def return_kernel(lat_size, lon_size, source_ref, out_ref, send_sem, recv_sem, own_sem):
    lat, lon = lax.axis_index("lat"), lax.axis_index("lon")
    before = (lax.rem(lat + lat_size - 1, lat_size), lax.rem(lon + lon_size - 1, lon_size))
    after = (lax.rem(lat + 1, lat_size), lax.rem(lon + 1, lon_size))
    sources = [(lat, before[1]), (before[0], lon), (before[0], before[1])]
    targets = [(lat, after[1]), (after[0], lon), (after[0], after[1])]
    barrier = pltpu.get_barrier_semaphore()
    for peer in targets + sources:
        pl.semaphore_signal(barrier, inc=1, device_id=peer, device_id_type=MESH)
    keep = pltpu.make_async_copy(source_ref.at[0], out_ref.at[3], own_sem)
    keep.start()
    pl.semaphore_wait(barrier, 6)
    copies = []
    for slot in (1, 2, 3):
        copies.append(
            pltpu.make_async_remote_copy(
                src_ref=source_ref.at[slot], dst_ref=out_ref.at[3 - slot],
                send_sem=send_sem.at[slot - 1], recv_sem=recv_sem.at[slot - 1],
                device_id=targets[slot - 1], device_id_type=MESH,
            )
        )
        copies[-1].start()
    keep.wait()
    for copy in copies:
        copy.wait()


def give_back(mesh_shape, attended):
    whole = pl.BlockSpec(memory_space=pltpu.VMEM)
    return pl.pallas_call(
        functools.partial(return_kernel, *mesh_shape),
        out_shape=jax.ShapeDtypeStruct(attended.shape, attended.dtype),
        in_specs=[whole],
        out_specs=whole,
        scratch_shapes=[
            pltpu.SemaphoreType.DMA((3,)),
            pltpu.SemaphoreType.DMA((3,)),
            pltpu.SemaphoreType.DMA,
        ],
        compiler_params=pltpu.CompilerParams(collective_id=1, has_side_effects=True),
    )(attended)


def unit(inputs):
    total = jnp.sum(inputs * inputs, axis=-1, keepdims=True)
    return (inputs * lax.rsqrt(total + 1e-06)).astype(jnp.bfloat16)


def block_kernel(
    lat_size, rolled_ref, local_ref, embed_ref, ebias_ref, egain_ref, eshift_ref, qkv_ref,
    scale_ref, bias_ref, attended_ref, tokens_ref,
):
    quads, rows, length = rolled_ref.shape
    count = quads * rows
    last = lax.axis_index("lat") == lat_size - 1

    def embed(ref):
        pre = dot_rows(ref[...].reshape(count, length), embed_ref[...]) + ebias_ref[...]
        return layer_norm(pre, egain_ref[...], eshift_ref[...]).astype(jnp.bfloat16)

    tokens = embed(rolled_ref)
    qkv = dot_plain(tokens, qkv_ref[...]).astype(jnp.bfloat16)
    tokens_ref[...] = embed(local_ref).reshape(tokens_ref.shape)
    batch = rows // 16
    qkv = qkv.reshape(quads, batch, 16, 3 * INNER)
    qkv = jnp.concatenate(
        [qkv[quad, sample] for sample in range(batch) for quad in range(quads)], axis=0
    )
    window = WIN * WIN
    one, two = iota((count, count), 0), iota((count, count), 1)
    apart = jnp.where(last, 1, 0) * jnp.abs((one % window) // 32 - (two % window) // 32)
    allowed = (one // window == two // window) & (apart == 0)
    for head in range(HEADS):
        lanes = head * HD
        query = unit(qkv[:, lanes : lanes + HD].astype(jnp.float32))
        key = unit(qkv[:, INNER + lanes : INNER + lanes + HD].astype(jnp.float32))
        value = qkv[:, 2 * INNER + lanes : 2 * INNER + lanes + HD]
        table = bias_ref[head]
        table = jnp.concatenate([table] * batch, axis=1)
        table = jnp.concatenate([table] * batch, axis=0)
        scores = dot_rows(query, key) * scale_ref[head] + table
        scores = jnp.where(allowed, scores, -1e30)
        expo = jnp.exp(scores - jnp.max(scores, axis=-1, keepdims=True))
        attn = (expo / jnp.sum(expo, axis=-1, keepdims=True)).astype(jnp.bfloat16)
        attended = dot_plain(attn, value).astype(jnp.bfloat16)
        for sample in range(batch):
            for quad in range(quads):
                start = sample * window + quad * 16
                attended_ref[quad, sample * 16 : sample * 16 + 16, lanes : lanes + HD] = attended[
                    start : start + 16
                ]


def final_kernel(attended_ref, tokens_ref, proj_ref, gain_ref, shift_ref, out_ref):
    quads, rows, inner = attended_ref.shape
    batch = rows // 16
    projected = dot_rows(attended_ref[...].reshape(quads * rows, inner), proj_ref[...])
    normed = layer_norm(projected, gain_ref[...], shift_ref[...])
    mixed = tokens_ref[...].reshape(quads * rows, D).astype(jnp.float32) + normed
    for quad in range(quads):
        for sample in range(batch):
            for r in range(HALF):
                start = quad * rows + sample * 16 + r * HALF
                col = quad % 2 * HALF
                out_ref[sample, quad // 2 * HALF + r, col : col + HALF, :] = mixed[
                    start : start + HALF
                ].astype(jnp.bfloat16)


def on_device(
    mesh_shape, field, embed_weight, embed_bias, embed_gain, embed_shift, qkv_weight,
    logit_scale, bias_table, proj_weight, post_gain, post_shift,
):
    batch = field.shape[0]
    per_quad = batch * 16
    length = VARS * PATCH * PATCH
    whole = pl.BlockSpec(memory_space=pltpu.VMEM)
    params = pltpu.CompilerParams(vmem_limit_bytes=VMEM_BYTES)
    scales = jnp.exp(jnp.minimum(logit_scale, scale_cap))
    bias = window_bias(bias_table)
    patches = pl.pallas_call(
        patch_kernel,
        out_shape=jax.ShapeDtypeStruct((QUADS, per_quad, length), jnp.bfloat16),
        in_specs=[whole],
        out_specs=whole,
        scratch_shapes=[pltpu.VMEM((batch * WIN * WIN, 16 * 128), jnp.float32)],
        compiler_params=params,
    )(field.transpose(0, 2, 1, 3))
    if mesh_shape == (4, 8):
        rolled, embed_all, qkv_all, proj_all = exchange(
            mesh_shape, patches, (embed_weight, qkv_weight, proj_weight)
        )
        embed_all = embed_all.reshape(D, -1)
        qkv_all = qkv_all.reshape(D, -1)
        proj_all = proj_all.reshape(D, -1)
    else:
        (rolled,) = exchange(mesh_shape, patches, ())
        embed_all, qkv_all, proj_all = (
            lax.all_gather(
                lax.all_gather(weight, "lon", axis=0, tiled=True), "lat", axis=0, tiled=True
            )
            for weight in (embed_weight, qkv_weight, proj_weight)
        )
    attended, tokens = pl.pallas_call(
        functools.partial(block_kernel, mesh_shape[0]),
        out_shape=[
            jax.ShapeDtypeStruct((QUADS, per_quad, INNER), jnp.bfloat16),
            jax.ShapeDtypeStruct((QUADS, per_quad, D), jnp.bfloat16),
        ],
        in_specs=[whole] * 7 + [pl.BlockSpec(memory_space=pltpu.SMEM), whole],
        out_specs=[whole] * 2,
        compiler_params=params,
    )(
        rolled, patches, embed_all, embed_bias.reshape(1, -1), embed_gain.reshape(1, -1),
        embed_shift.reshape(1, -1), qkv_all, scales, bias,
    )
    attended = give_back(mesh_shape, attended)
    return pl.pallas_call(
        final_kernel,
        out_shape=jax.ShapeDtypeStruct((batch, WIN, WIN, D), jnp.bfloat16),
        in_specs=[whole] * 5,
        out_specs=whole,
        compiler_params=params,
    )(attended, tokens, proj_all, post_gain.reshape(1, -1), post_shift.reshape(1, -1))


def solution(mesh):
    placed = (
        P(None, None, "lat", "lon"),
        P(("lat", "lon"), None),
        P(),
        P(),
        P(),
        P(("lat", "lon"), None),
        P(),
        P(),
        P(("lat", "lon"), None),
        P(),
        P(),
    )
    return jax.shard_map(
        functools.partial(on_device, (mesh.shape["lat"], mesh.shape["lon"])),
        mesh=mesh,
        in_specs=placed,
        out_specs=P(None, "lat", "lon", None),
        check_vma=False,
    )
```

time: 243 us -> 128 us (0.53)
  waiting for transfers between devices: 122 us -> 0 us
  Pallas kernels: 0 us -> 115 us
  blocking collectives: 36.3 us -> 0 us
  local copies, waits for them, and re-layouts: 40.2 us -> 7.84 us
  matrix products: 17.9 us -> 4.28 us
  between operations: 13.5 us -> 0.07 us
  other arithmetic: 8.76 us -> 0.73 us
  starting transfers between devices: 3.45 us -> 0 us
    pallas_call x0 -> x5, Pallas kernels: none -> 115 us  [the longest x1 77.2 us: exchange(): pl.pallas_call(functools.partial(exchange_kernel, lat_size, lon_size, wei...]
    all_gather x4 -> x0, waiting for transfers between devices: 89.6 us -> none  [the longest x1 56.5 us: on_device(): lax.all_gather(qkv_band, 'lat', axis=0, tiled=True)]
    all_gather x2 -> x0, blocking collectives: 36.3 us -> none  [the longest x1 20.4 us: on_device(): lax.all_gather(embed_weight, 'lon', axis=0, tiled=True)]
    ppermute x4 -> x0, waiting for transfers between devices: 32 us -> none  [shifted(): return lax.ppermute(value, axis, pairs)]
    reshape x2 -> x5, local copies, waits for them, and re-layouts: 28.1 us -> 3 us  [the longest x1 0.61 us: on_device(): post_gain.reshape(1, -1)]
    dot_general x5 -> x0, matrix products: 13.8 us -> none  [the longest x2 5.88 us: dot_rows(): lax.dot_general(left, right, (((1,), (1,)), ((), ())), preferred_element_...]
    ppermute x4 -> x0, starting transfers between devices: 3.33 us -> none  [shifted(): return lax.ppermute(value, axis, pairs)]
    another operation x2 -> x0, local copies, waits for them, and re-layouts: 3.31 us -> none  [the longest x1 2.84 us: attend(): kv_win = to_windows(kv_block, WIN).reshape(-1, WIN * WIN, 2, HEADS, HD)]
  transfers between devices with their start and end apart: 8 -> 0, of which waited for: 8 -> 0; matrix products, arithmetic and copies ran while one was open for 23% -> 0% of each run, Pallas kernels for 0% -> 0%
where the time goes in v1:
time: 128 us
  Pallas kernels  115 us (90%)
  local copies, waits for them, and re-layouts  7.84 us (6%)
  matrix products  4.28 us (3%)
    pallas_call x1, Pallas kernels, exchange(): pl.pallas_call(functools.partial(exchange_kernel, lat_size, lon_size, wei...  77.2 us
    pallas_call x1, Pallas kernels, on_device(): pl.pallas_call(functools.partial(block_kernel, mesh_shape[0]), out_shape=...  15.6 us
    pallas_call x1, Pallas kernels, give_back(): pl.pallas_call(functools.partial(return_kernel, *mesh_shape), out_shape=j...  10.5 us
    pallas_call x1, Pallas kernels, on_device(): pl.pallas_call(patch_kernel, out_shape=jax.ShapeDtypeStruct((QUADS, per_q...  7.03 us
    pallas_call x1, Pallas kernels, on_device(): pl.pallas_call(final_kernel, out_shape=jax.ShapeDtypeStruct((batch, WIN,...  4.34 us
    dot_general x1, matrix products, window_bias(): jnp.einsum('hrc,qkc->hqkr', table, col_onehot, precision=lax.Precision.HI...  4.28 us
    unnamed x15, local copies, waits for them, and re-layouts  3.95 us

profile of v1, /device:TPU:0, one launch (start us, length us, event | category | flops | bytes accessed | tf_op | source)
XLA Modules:
  0.0 127.5 jit_solution(6194444680027909569)
XLA Ops:
  0.0 0.0 copy-start.5
  0.0 0.0 copy-start
  0.0 0.0 copy-start.1
  0.0 0.0 copy-start.2
  0.0 0.0 copy-start.6
  0.0 3.9 %copy.13 = bf16[4,70,32,32]{3,1,2,0:T(8,128)(2,1)} copy(bf16[4,70,32,32]{1,3,2,0:T(8,128)(2,1)} %param.11) | data formatting | bytes 1146880 | tf_op args[0]
  3.9 7.0 %shard_map.109.patch_ref.local_ref = bf16[4,64,1120]{2,1,0:T(8,128)(2,1)} custom-call(bf16[4,32,70,32]{3,2,1,0:T(8,128)(2,1)} %bitcast.15), custom_call_target="tpu_custom_call" | custom-call | tf_op jit(solution)/shard_map/pallas_call | solution.py:356
  11.0 77.2 %shard_map.110 = (bf16[4,64,1120]{2,1,0:T(8,128)(2,1)}, bf16[32,48,1120]{2,1,0:T(8,128)(2,1)}, bf16[32,48,2304]{2,1,0:T(8,128)(2,1)}, bf16[32,48,768]{2,1,0:T(8,128)(2,1)}) custom-call(bf16[4,64,1120]{2,1,0:T(8,128)(2,1)} %shard_map.109.patch_ref.local_ref, bf16[48,1120]{1,0:T(8,128)(2,1)} %refs_0_.1, bf16[48,2304]{1,0:T(8,128)(2,1)} %refs_1_.1, ...), custom_call_target="tpu_custom_call" | custom-call | tf_op jit(solution)/shard_map/pallas_call | solution.py:221
  88.2 0.1 subtract_add_fusion
  88.3 0.1 subtract_add_fusion.1
  88.4 0.0 copy-done.5
  88.4 4.3 %multiply_reduce_fusion = f32[64,64,12]{1,2,0:T(8,128)S(1)} fusion(f32[64,64,15]{1,2,0:T(8,128)S(1)} %fusion.2, s32[64,64]{1,0:T(8,128)S(1)} %subtract_add_fusion.1, f32[12,15,15]{2,1,0:T(8,128)S(1)} %copy-done.5), kind=kOutput, calls=%fused_computation | convolution fusion | flops 134208048 | bytes 469552 | tf_op jit(solution)/shard_map/hrc,qkc->hqkr/dot_general | solution.py:65
  92.7 0.9 copy.17
  93.6 0.0 copy-done
  93.6 0.6 reshape.241.ebias_ref
  94.2 0.0 copy-done.1
  94.2 0.6 reshape.242.egain_ref
  94.8 0.0 copy-done.2
  94.8 0.6 reshape.243.eshift_ref
  95.4 0.0 copy-done.6
  95.4 0.5 minimum_exponential_fusion.scale_ref
  95.9 0.0 copy-start.3
  95.9 0.0 copy-start.4
  95.9 15.6 %shard_map.111 = (bf16[4,64,768]{2,1,0:T(8,128)(2,1)}, bf16[4,64,1536]{2,1,0:T(8,128)(2,1)}) custom-call(bf16[4,64,1120]{2,1,0:T(8,128)(2,1)} %get-tuple-element.11.rolled_ref, bf16[4,64,1120]{2,1,0:T(8,128)(2,1)} %shard_map.109.patch_ref.local_ref, bf16[1536,1120]{1,0:T(8,128)(2,1)} %bitcast.17, f32[1,1536]{1,0:T(1,128)} %reshape.241.ebias_ref, ...), custom_call_target="tpu_custom_call" | custom-call | tf_op jit(solution)/shard_map/pallas_call | solution.py:379
  111.5 10.5 %shard_map.112.attended_ref = bf16[4,64,768]{2,1,0:T(8,128)(2,1)} custom-call(bf16[4,64,768]{2,1,0:T(8,128)(2,1)} %get-tuple-element.14.source_ref), custom_call_target="tpu_custom_call" | custom-call | tf_op jit(solution)/shard_map/pallas_call | solution.py:265
  122.0 0.0 copy-done.3
  122.0 0.6 reshape.246.gain_ref
  122.6 0.0 copy-done.4
  122.6 0.6 reshape.247.shift_ref
  123.2 4.3 %shard_map.113 = bf16[4,8,8,1536]{3,2,1,0:T(8,128)(2,1)} custom-call(bf16[4,64,768]{2,1,0:T(8,128)(2,1)} %shard_map.112.attended_ref, bf16[4,64,1536]{2,1,0:T(8,128)(2,1)} %get-tuple-element.15.tokens_ref, bf16[1536,768]{1,0:T(8,128)(2,1)} %bitcast.18, f32[1,1536]{1,0:T(1,128)} %reshape.246.gain_ref, f32[1,1536]{1,0:T(1,128)} %reshape.247.shift_ref), custom_call_target="tpu_custom_call" | custom-call | tf_op jit(solution)/shard_map/pallas_call | solution.py:393
  (3 shorter events, 0.1 us)
Async XLA Ops:
  0.0 88.4 %copy-start.5 = (f32[12,15,15]{2,1,0:T(8,128)S(1)}, f32[12,15,15]{2,1,0:T(8,128)}, u32[]{:S(2)}) copy-start(f32[12,15,15]{2,1,0:T(8,128)} %param.18) | copy-start | bytes 32404
  0.0 93.6 %copy-start = (f32[1536]{0:T(1024)S(1)}, f32[1536]{0:T(1024)}, u32[]{:S(2)}) copy-start(f32[1536]{0:T(1024)} %param.13) | copy-start | bytes 18436
  0.0 94.2 %copy-start.1 = (f32[1536]{0:T(1024)S(1)}, f32[1536]{0:T(1024)}, u32[]{:S(2)}) copy-start(f32[1536]{0:T(1024)} %param.14) | copy-start | bytes 18436
  0.0 94.8 %copy-start.2 = (f32[1536]{0:T(1024)S(1)}, f32[1536]{0:T(1024)}, u32[]{:S(2)}) copy-start(f32[1536]{0:T(1024)} %param.15) | copy-start | bytes 18436
  0.0 95.4 %copy-start.6 = (f32[12]{0:T(128)S(1)}, f32[12]{0:T(128)}, u32[]{:S(2)}) copy-start(f32[12]{0:T(128)} %param.17) | copy-start | bytes 148
  95.9 26.1 %copy-start.3 = (f32[1536]{0:T(1024)S(1)}, f32[1536]{0:T(1024)}, u32[]{:S(2)}) copy-start(f32[1536]{0:T(1024)} %param.20) | copy-start | bytes 18436
  95.9 26.7 %copy-start.4 = (f32[1536]{0:T(1024)S(1)}, f32[1536]{0:T(1024)}, u32[]{:S(2)}) copy-start(f32[1536]{0:T(1024)} %param.21) | copy-start | bytes 18436

commit v2 on v0

v2 whole, which is shorter than its diff:
```python
import functools
import math

import jax
import jax.numpy as jnp
from jax import lax
from jax.experimental import pallas as pl
from jax.experimental.pallas import tpu as pltpu
from jax.sharding import PartitionSpec as P

VARS = 70
PATCH = 4
D = 1536
HEADS = 12
HD = 64
WIN = 8
HALF = WIN // 2
QUADS = 4
INNER = HEADS * HD

MESH = pl.DeviceIdType.MESH
VMEM_BYTES = 56 * 1024 * 1024

scale_cap = math.log(100.0)


def layer_norm(inputs, gain, shift):
    average = jnp.mean(inputs, axis=-1, keepdims=True)
    centred = inputs - average
    spread = jnp.mean(centred * centred, axis=-1, keepdims=True)
    return centred * lax.rsqrt(spread + 1e-05) * gain + shift


def dot_rows(left, right):
    return lax.dot_general(
        left, right, (((1,), (1,)), ((), ())), preferred_element_type=jnp.float32
    )


def dot_plain(left, right):
    return lax.dot_general(
        left, right, (((1,), (0,)), ((), ())), preferred_element_type=jnp.float32
    )


def iota(shape, dim):
    return lax.broadcasted_iota(jnp.int32, shape, dim)


def onehot(condition):
    return jnp.where(condition, 1.0, 0.0).astype(jnp.bfloat16)


def bias_into(table_ref, padded, bias):
    heads = table_ref.shape[0]
    span = 2 * WIN - 1
    padded[...] = jnp.zeros_like(padded)
    for level in range(span):
        padded[0:heads, level * 16 : level * 16 + span] = table_ref[:, level, :]
    table = 16.0 * jax.nn.sigmoid(padded[...])
    high = table.astype(jnp.bfloat16)
    rest = table - high.astype(jnp.float32)
    middle = rest.astype(jnp.bfloat16)
    low = (rest - middle.astype(jnp.float32)).astype(jnp.bfloat16)
    parts = jnp.concatenate([high, middle, low], axis=0)
    places = WIN * WIN
    entry = iota((256, places), 0)
    key = iota((256, places), 1)
    key_row = key // 32 * HALF + key % 16 // HALF
    key_col = key // 16 % 2 * HALF + key % HALF
    for query in range(places):
        row = query // 32 * HALF + query % 16 // HALF
        col = query // 16 % 2 * HALF + query % HALF
        wanted = (row + WIN - 1 - key_row) * 16 + (col + WIN - 1 - key_col)
        found = dot_plain(parts, onehot(entry == wanted))
        bias[query] = found[0:16] + found[16:32] + found[32:48]


def patch_into(field_ref, spread, out):
    batch = field_ref.shape[0]
    spread[...] = jnp.zeros_like(spread)
    side = WIN * PATCH
    pick_row = iota((side, side), 0)
    pick_col = iota((side, side), 1)
    pick = onehot(pick_col == (pick_row % WIN) * PATCH + pick_row // WIN)
    for sample in range(batch):
        for row in range(side):
            i, p = row // PATCH, row % PATCH
            picked = dot_plain(pick, field_ref[sample, row])
            for q in range(PATCH):
                lane = (p * PATCH + q) * 128
                spread[pl.ds((sample * WIN + i) * WIN, WIN), lane : lane + VARS] = picked[
                    q * WIN : (q + 1) * WIN
                ]
    tokens = batch * WIN * WIN
    to = iota((tokens, tokens), 0)
    source = iota((tokens, tokens), 1)
    per_quad = batch * 16
    quad, sample, place = to // per_quad, to % per_quad // 16, to % 16
    row = quad // 2 * HALF + place // HALF
    col = quad % 2 * HALF + place % HALF
    order = onehot(source == (sample * WIN + row) * WIN + col)
    length = VARS * PATCH * PATCH
    feature = iota((128, length), 1)
    same = feature // 16 == iota((128, length), 0)
    slot = feature % 16
    total = jnp.zeros((tokens, length), jnp.float32)
    for pq in range(16):
        piece = spread[:, pq * 128 : (pq + 1) * 128].astype(jnp.bfloat16)
        total = total + dot_plain(piece, onehot(same & (slot == pq)))
    out[...] = dot_plain(order, total.astype(jnp.bfloat16)).astype(jnp.bfloat16).reshape(out.shape)


def unit(inputs):
    total = jnp.sum(inputs * inputs, axis=-1, keepdims=True)
    return (inputs * lax.rsqrt(total + 1e-06)).astype(jnp.bfloat16)


E, Q, J = 0, 1, 2

STEPS = (
    "patch X00 Y00 Z01".split() + "X10 Y10 Z02 X20".split() + "Y20 Z03 X01 Y01".split()
    + "bias X02 Y02 Z11".split() + "X03 Y03 Z12".split() + "D00 D01 D02 D03".split()
    + "local X11 Y11 rolled".split() + "Z13 X12 Y12 Z21".split() + "Z22 Z23 X13 Y13".split()
    + "D10 X21 Y21 D11".split() + "X22 Y22 D12 X23".split() + "Y23 D13 qkv attend".split()
    + "D20 D21 D22 D23".split() + "final".split()
)


def whole_kernel(
    lat_size, lon_size, gather, field_ref, embed_ref, qkv_ref, proj_ref, ebias_ref, egain_ref,
    eshift_ref, scale_ref, table_ref, pgain_ref, pshift_ref, out_ref, embed_all, qkv_all,
    proj_all, spread, patches, rolled, tokens, moved, qkv, attended, returned, padded, bias,
    send_sem, recv_sem, own_sem,
):
    local, outs = (embed_ref, qkv_ref, proj_ref), (embed_all, qkv_all, proj_all)
    lat, lon = lax.axis_index("lat"), lax.axis_index("lon")
    before = (lax.rem(lat + lat_size - 1, lat_size), lax.rem(lon + lon_size - 1, lon_size))
    after = (lax.rem(lat + 1, lat_size), lax.rem(lon + 1, lon_size))
    backward = [(lat, before[1]), (before[0], lon), (before[0], before[1])]
    forward = [(lat, after[1]), (after[0], lon), (after[0], after[1])]
    y, x = lat // 2, lax.rem(lat, 2)
    z, core = lon // 2, lax.rem(lon, 2)
    greeted = backward + forward
    depth = lon_size // 2
    if gather:
        lat_x = y * 2 + 1 - x
        lat_y = (1 - y) * 2 + x
        lat_d = (1 - y) * 2 + 1 - x
        to_x, to_y, to_c = (lat_x, lon), (lat_y, lon), (lat, z * 2 + 1 - core)
        to_z = [(lat, lax.rem(z + k, depth) * 2 + core) for k in range(depth)]
        greeted = greeted + [to_x, to_y, to_c] + to_z[1:]
    barrier = pltpu.get_barrier_semaphore()
    for peer in greeted:
        pl.semaphore_signal(barrier, inc=1, device_id=peer, device_id_type=MESH)
    me = lat * lon_size + lon
    keeps = []
    for t in (E, Q, J):
        keep = outs[t].at[me] if gather else outs[t]
        keeps.append(pltpu.make_async_copy(local[t], keep, own_sem.at[t]))
    for keep in keeps:
        keep.start()
    pl.semaphore_wait(barrier, len(greeted))

    count = [0]
    started = []

    def send(src, dst, landing, device):
        index = count[0]
        count[0] += 1

        def copy(to):
            return pltpu.make_async_remote_copy(
                src_ref=src, dst_ref=to, send_sem=send_sem.at[index],
                recv_sem=recv_sem.at[index], device_id=device, device_id_type=MESH,
            )

        going = copy(dst)
        going.start()
        started.append(going)
        return copy(landing)

    def at(row, k, sibling=False):
        side = 1 - core if sibling else core
        return row * lon_size + lax.rem(z + depth - k, depth) * 2 + side

    z_in, x_in, y_in, d_in, c_in = {}, {}, {}, {}, {E: [], Q: [], J: []}

    def across(t, row, k, src):
        dst = outs[t].at[at(row, k)]
        c_in[t].append(send(src, dst, outs[t].at[at(row, k, True)], to_c))

    def fan(t, k, src):
        dst = outs[t].at[at(lat, k)]
        x_in[t, k] = send(src, dst, outs[t].at[at(lat_x, k)], to_x)
        y_in[t, k] = send(src, dst, outs[t].at[at(lat_y, k)], to_y)
        across(t, lat, k, src)

    def pass_on(kind, t, k):
        rows = outs[t].shape[1]
        cut = rows // 3 // 16 * 16 * (1 + k % 2)
        far = outs[t].at[at(lat_d, k)]
        if kind == "Z":
            z_in[t, k].wait_recv()
            fan(t, k, outs[t].at[at(lat, k)])
        elif kind == "X":
            x_in[t, k].wait_recv()
            block = outs[t].at[at(lat_x, k)]
            part = block.at[0:cut]
            d_in[t, k, 0] = send(part, part, far.at[0:cut], to_y)
            across(t, lat_x, k, block)
        elif kind == "Y":
            y_in[t, k].wait_recv()
            block = outs[t].at[at(lat_y, k)]
            part = block.at[cut:rows]
            d_in[t, k, 1] = send(part, part, far.at[cut:rows], to_x)
            across(t, lat_y, k, block)
        else:
            d_in[t, k, 0].wait_recv()
            d_in[t, k, 1].wait_recv()
            across(t, lat_d, k, far)

    def have(t):
        keeps[t].wait()
        for copy in c_in[t]:
            copy.wait_recv()

    if gather:
        for t in (E, Q, J):
            for k in range(1, depth):
                z_in[t, k] = send(local[t], outs[t].at[me], outs[t].at[at(lat, k)], to_z[k])
            fan(t, 0, local[t])

    quads, rows, length = patches.shape
    batch = rows // 16
    window = WIN * WIN
    total = quads * rows
    halo = []

    def embed(ref, into):
        weight = embed_all[...].reshape(D, length)
        pre = dot_rows(ref[...].reshape(total, length), weight) + ebias_ref[...].reshape(1, D)
        gain, shift = egain_ref[...].reshape(1, D), eshift_ref[...].reshape(1, D)
        into[...] = layer_norm(pre, gain, shift).astype(jnp.bfloat16)

    def attend():
        last = lat == lat_size - 1
        one, two = iota((total, total), 0), iota((total, total), 1)
        apart = jnp.where(last, 1, 0) * jnp.abs((one % window) // 32 - (two % window) // 32)
        allowed = (one // window == two // window) & (apart == 0)
        for head in range(HEADS):
            lanes = head * HD
            query = unit(qkv[:, lanes : lanes + HD].astype(jnp.float32))
            key = unit(qkv[:, INNER + lanes : INNER + lanes + HD].astype(jnp.float32))
            value = qkv[:, 2 * INNER + lanes : 2 * INNER + lanes + HD]
            near = bias[:, head, :]
            near = jnp.concatenate([near] * batch, axis=1)
            near = jnp.concatenate([near] * batch, axis=0)
            scale = jnp.exp(jnp.minimum(jnp.full((1, total), scale_ref[head]), scale_cap))
            scores = dot_rows(query, key) * scale + near
            scores = jnp.where(allowed, scores, -1e30)
            expo = jnp.exp(scores - jnp.max(scores, axis=-1, keepdims=True))
            attn = (expo / jnp.sum(expo, axis=-1, keepdims=True)).astype(jnp.bfloat16)
            result = dot_plain(attn, value).astype(jnp.bfloat16)
            for sample in range(batch):
                for quad in range(quads):
                    start = sample * window + quad * 16
                    attended[quad, sample * 16 : sample * 16 + 16, lanes : lanes + HD] = result[
                        start : start + 16
                    ]

    backs = []
    for step in STEPS:
        if step == "patch":
            patch_into(field_ref, spread, patches)
            for slot in (1, 2, 3):
                halo.append(
                    send(patches.at[3 - slot], rolled.at[slot], rolled.at[slot], backward[slot - 1])
                )
            rolled[0] = patches[3]
        elif step == "bias":
            bias_into(table_ref, padded, bias)
        elif step == "local":
            have(E)
            embed(patches, tokens)
        elif step == "rolled":
            for copy in halo:
                copy.wait_recv()
            embed(rolled, moved)
        elif step == "qkv":
            have(Q)
            part = dot_plain(moved[...], qkv_all[...].reshape(D, 3 * INNER)).astype(jnp.bfloat16)
            for quad in range(quads):
                for sample in range(batch):
                    start = quad * rows + sample * 16
                    to = sample * window + quad * 16
                    qkv[to : to + 16, :] = part[start : start + 16]
        elif step == "attend":
            attend()
            for slot in (1, 2, 3):
                landing = returned.at[3 - slot]
                backs.append(send(attended.at[slot], landing, landing, forward[slot - 1]))
            returned[3] = attended[0]
        elif step == "final":
            have(J)
            for copy in backs:
                copy.wait_recv()
            weight = proj_all[...].reshape(D, INNER)
            projected = dot_rows(returned[...].reshape(total, INNER), weight)
            gain, shift = pgain_ref[...].reshape(1, D), pshift_ref[...].reshape(1, D)
            mixed = tokens[...].astype(jnp.float32) + layer_norm(projected, gain, shift)
            for quad in range(quads):
                for sample in range(batch):
                    for r in range(HALF):
                        start = quad * rows + sample * 16 + r * HALF
                        col = quad % 2 * HALF
                        out_ref[sample, quad // 2 * HALF + r, col : col + HALF, :] = mixed[
                            start : start + HALF
                        ].astype(jnp.bfloat16)
        elif gather:
            pass_on(step[0], int(step[1]), int(step[2]))
    for copy in started:
        copy.wait_send()


def on_device(
    mesh_shape, field, embed_weight, embed_bias, embed_gain, embed_shift, qkv_weight,
    logit_scale, bias_table, proj_weight, post_gain, post_shift,
):
    batch = field.shape[0]
    per_quad = batch * 16
    total = QUADS * per_quad
    length = VARS * PATCH * PATCH
    whole = pl.BlockSpec(memory_space=pltpu.VMEM)
    anywhere = pl.BlockSpec(memory_space=pl.ANY)
    weights = (embed_weight, qkv_weight, proj_weight)
    gather = mesh_shape == (4, 8)
    devices = mesh_shape[0] * mesh_shape[1]
    if gather:
        blocks = [(devices,) + weight.shape for weight in weights]
    else:
        weights = [
            lax.all_gather(
                lax.all_gather(weight, "lon", axis=0, tiled=True), "lat", axis=0, tiled=True
            )
            for weight in weights
        ]
        blocks = [weight.shape for weight in weights]
    copies = 6 + (3 * 35 if gather else 0)
    bf16, f32 = jnp.bfloat16, jnp.float32
    return pl.pallas_call(
        functools.partial(whole_kernel, mesh_shape[0], mesh_shape[1], gather),
        out_shape=jax.ShapeDtypeStruct((batch, WIN, WIN, D), bf16),
        in_specs=[whole] + [anywhere] * 3 + [whole] * 3
        + [pl.BlockSpec(memory_space=pltpu.SMEM)] + [whole] * 3,
        out_specs=whole,
        scratch_shapes=[pltpu.VMEM(shape, bf16) for shape in blocks]
        + [
            pltpu.VMEM((total, 16 * 128), f32),
            pltpu.VMEM((QUADS, per_quad, length), bf16),
            pltpu.VMEM((QUADS, per_quad, length), bf16),
            pltpu.VMEM((total, D), bf16),
            pltpu.VMEM((total, D), bf16),
            pltpu.VMEM((total, 3 * INNER), bf16),
            pltpu.VMEM((QUADS, per_quad, INNER), bf16),
            pltpu.VMEM((QUADS, per_quad, INNER), bf16),
            pltpu.VMEM((16, 256), f32),
            pltpu.VMEM((WIN * WIN, 16, WIN * WIN), f32),
            pltpu.SemaphoreType.DMA((copies,)),
            pltpu.SemaphoreType.DMA((copies,)),
            pltpu.SemaphoreType.DMA((3,)),
        ],
        compiler_params=pltpu.CompilerParams(
            collective_id=0, has_side_effects=True, vmem_limit_bytes=VMEM_BYTES
        ),
    )(
        field.transpose(0, 2, 3, 1), *weights, embed_bias, embed_gain, embed_shift, logit_scale,
        bias_table, post_gain, post_shift,
    )


def solution(mesh):
    placed = (
        P(None, None, "lat", "lon"),
        P(("lat", "lon"), None),
        P(),
        P(),
        P(),
        P(("lat", "lon"), None),
        P(),
        P(),
        P(("lat", "lon"), None),
        P(),
        P(),
    )
    return jax.shard_map(
        functools.partial(on_device, (mesh.shape["lat"], mesh.shape["lon"])),
        mesh=mesh,
        in_specs=placed,
        out_specs=P(None, "lat", "lon", None),
        check_vma=False,
    )
```

time: 243 us -> 88.2 us (0.36)
  waiting for transfers between devices: 122 us -> 0 us
  Pallas kernels: 0 us -> 85.9 us
  local copies, waits for them, and re-layouts: 40.2 us -> 2.06 us
  blocking collectives: 36.3 us -> 0 us
  matrix products: 17.9 us -> 0 us
  between operations: 13.5 us -> 0.01 us
  other arithmetic: 8.76 us -> 0 us
  starting transfers between devices: 3.45 us -> 0 us
    all_gather x4 -> x0, waiting for transfers between devices: 89.6 us -> none  [the longest x1 56.5 us: on_device(): lax.all_gather(qkv_band, 'lat', axis=0, tiled=True)]
    pallas_call x0 -> x1, Pallas kernels: none -> 85.9 us  [on_device(): pl.pallas_call(functools.partial(whole_kernel, mesh_shape[0], mesh_shape[...]
    all_gather x2 -> x0, blocking collectives: 36.3 us -> none  [the longest x1 20.4 us: on_device(): lax.all_gather(embed_weight, 'lon', axis=0, tiled=True)]
    ppermute x4 -> x0, waiting for transfers between devices: 32 us -> none  [shifted(): return lax.ppermute(value, axis, pairs)]
    reshape x2 -> x0, local copies, waits for them, and re-layouts: 28.1 us -> none  [the longest x1 15 us: on_device(): field.reshape(batch, VARS, tile_rows, PATCH, tile_cols, PATCH)]
    dot_general x6 -> x0, matrix products: 17.9 us -> none  [the longest x2 5.88 us: dot_rows(): lax.dot_general(left, right, (((1,), (1,)), ((), ())), preferred_element_...]
    unnamed x31 -> x1, local copies, waits for them, and re-layouts: 5.52 us -> 2.06 us
    ppermute x4 -> x0, starting transfers between devices: 3.33 us -> none  [shifted(): return lax.ppermute(value, axis, pairs)]
  transfers between devices with their start and end apart: 8 -> 0, of which waited for: 8 -> 0; matrix products, arithmetic and copies ran while one was open for 23% -> 0% of each run, Pallas kernels for 0% -> 0%
where the time goes in v2:
time: 88.2 us; the launch traced here: 88 us
  Pallas kernels  85.9 us (97%)
  local copies, waits for them, and re-layouts  2.06 us (2%)
    pallas_call x1, Pallas kernels, on_device(): pl.pallas_call(functools.partial(whole_kernel, mesh_shape[0], mesh_shape[...  85.9 us
    unnamed x1, local copies, waits for them, and re-layouts  2.06 us

profile of v2, /device:TPU:0, one launch (start us, length us, event | category | flops | bytes accessed | tf_op | source)
XLA Modules:
  0.0 88.0 jit_solution(462556254442563815)
XLA Ops:
  0.0 85.9 %shard_map.109 = bf16[4,8,8,1536]{3,2,1,0:T(8,128)(2,1)} custom-call(bf16[4,32,32,70]{3,2,1,0:T(8,128)(2,1)} %bitcast.1, bf16[48,1120]{1,0:T(8,128)(2,1)} %embed_ref.1, bf16[48,2304]{1,0:T(8,128)(2,1)} %qkv_ref.1, bf16[48,768]{1,0:T(8,128)(2,1)} %proj_ref.1, f32[1536]{0:T(1024)} %ebias_ref.1, f32[1536]{0:T(1024)} %egain_ref.1, f32[1536]{0:T(1024)} %eshift_ref.1, ...), custom_call_target="tpu_custom_call" | custom-call | tf_op jit(solution)/shard_map/pallas_call | solution.py:351
  85.9 2.1 %copy.13 = bf16[4,8,8,1536]{3,2,1,0:T(8,128)(2,1)} copy(bf16[4,8,8,1536]{3,2,1,0:T(8,128)(2,1)} %shard_map.109) | data formatting | bytes 1572864
